TPU v7x, 512 devices: a whole 4x8x8 slice. The times are simulated.
512 devices in a mesh: col: 128 (over z, y, core), row: 4 (over x).
Axes of the slice: x: 4, y: 8, z: 8, core: 2. Of those that a mesh axis runs over, the one named last changes fastest.
Arguments:
- panel: int32 [128], replicated, may hold values from 0 to 127, each once
- centres_cols: bfloat16 [65536, 1024], P('col'), may hold values from -1 to 1
- centres_rows: bfloat16 [2048, 1024], P(('row', 'col')), may hold values from -1 to 1
- diag_inverse: float32 [65536, 512], P('col'), as said below
- trailing: float32 [2048, 65536], P('row', 'col'), may hold values from -6 to 6
Outputs:
- updated: float32 [2048, 65536], P('row', 'col')
Inputs may be any that keep to these rules, and one draw needn't show every extreme that they name: panel holds each of 0 to 127 once. Each 512 x 512 block of diag_inverse is lower triangular with a positive diagonal.
All inputs are finite; a program needn't handle non-finite values.
Results may differ from a plain program's by a relative error of at most 0.0003.
Values may be sent and summed in bfloat16 or wider, within the bound.
No kernel may reach another device: no remote copies, remote signals or barrier semaphores. Data moves between devices by JAX's collectives and lax.ppermute only.
A program may use at most 64 MiB of HBM per device.

v0:
```python
import math
import jax
import jax.numpy as jnp
from jax import lax
from jax.sharding import PartitionSpec as P

LAYERS = 3


def broadcast(shard, axis, root):
    mine = lax.axis_index(axis) == root
    return lax.psum(jnp.where(mine, shard, jnp.zeros_like(shard)), axis)


def kernel(left, right):
    gram = lax.dot_general(
        left, right, (((1,), (1,)), ((), ())), preferred_element_type=jnp.float32
    )
    left_f = left.astype(jnp.float32)
    right_f = right.astype(jnp.float32)
    inv_left = 1.0 / jnp.sqrt(jnp.sum(left_f * left_f, axis=1) + 1e-06)
    inv_right = 1.0 / jnp.sqrt(jnp.sum(right_f * right_f, axis=1) + 1e-06)
    cosine = gram * inv_left[:, None] * inv_right[None, :]
    theta = cosine
    rho_now = cosine
    for layer in range(LAYERS):
        angle_now = jnp.arccos(rho_now)
        zero_order = (math.pi - angle_now) / math.pi
        rho_next = (jnp.sqrt(1.0 - rho_now * rho_now) + (math.pi - angle_now) * rho_now) / math.pi
        theta = theta * zero_order + rho_next
        rho_now = rho_next
    return theta / (inv_left[:, None] * inv_right[None, :])


def apply_inverse(values, inverse):
    return lax.dot_general(
        values,
        inverse,
        (((1,), (1,)), ((), ())),
        precision=lax.Precision.HIGHEST,
        preferred_element_type=jnp.float32,
    )


def on_device(panel, centres_cols, centres_rows, diag_inverse, trailing):
    col_count = lax.axis_size("col")
    target_rank = col_count // 4
    block_ids = jnp.arange(col_count, dtype=jnp.int32)
    panel_at = jnp.sum(jnp.where(panel == target_rank, block_ids, 0))
    panel_x = broadcast(centres_cols, "col", panel_at)
    panel_inv = broadcast(diag_inverse, "col", panel_at)

    def panel_rows_of(piece):
        return apply_inverse(kernel(piece, panel_x), panel_inv)

    rows_l = panel_rows_of(lax.all_gather(centres_rows, "col", axis=0, tiled=True))
    cols_l = panel_rows_of(centres_cols)
    update = lax.dot_general(
        rows_l,
        cols_l,
        (((1,), (1,)), ((), ())),
        precision=lax.Precision.HIGHEST,
        preferred_element_type=jnp.float32,
    )
    block_here = lax.axis_index("col")
    own_rank = lax.dynamic_index_in_dim(panel, block_here, 0, keepdims=False)
    return jnp.where(own_rank > target_rank, trailing - update, trailing)


def solution(mesh):
    return jax.shard_map(
        on_device,
        mesh=mesh,
        in_specs=(P(), P("col", None), P(("row", "col"), None), P("col", None), P("row", "col")),
        out_specs=P("row", "col"),
        check_vma=False,
    )
```

profile of v0, /device:TPU:1, one launch (start us, length us, event | category | flops | bytes accessed | tf_op | source)
XLA Modules:
  0.0 512.0 jit_solution(12042767771723486847)
XLA Ops:
  6.5 0.0 all-reduce.3.cloned.1.call-start
  6.5 1.3 fusion.110
  8.5 1.1 broadcast_select_fusion
  9.5 0.0 copy-start.2
  9.6 0.0 all-reduce.3.cloned.1.call-update
  9.6 0.0 all-reduce.5.cloned.1.call-start
  9.6 1.1 copy-done.2
  10.8 1.1 broadcast_select_fusion.1
  11.8 0.0 copy-start.5
  11.8 0.0 copy-start
  11.8 0.0 all-reduce.5.cloned.1.call-update
  11.9 0.0 all-gather.3.cloned.1.call-start
  11.9 0.7 all-gather.3.cloned.1.call-update
  12.6 0.0 copy-done.5
  12.6 0.6 dynamic_slice.4
  13.8 0.0 copy-done
  13.9 0.3 multiply_reduce_fusion
  14.1 197.4 %all-reduce.3.cloned.1.call-done = bf16[512,1024]{1,0:T(8,128)(2,1)} async-done(((bf16[512,1024]{1,0:T(8,128)(2,1)}), bf16[512,1024]{1,0:T(8,128)(2,1)}) %all-reduce.3.cloned.1.call-update) | async-done | bytes 1048592 | tf_op jit(solution)/shard_map/psum | solution.py:12
  211.6 0.0 copy-start.3
  211.6 1.6 multiply_reduce_fusion.1
  213.2 0.0 copy-done.3
  213.2 0.7 fusion.1
  213.9 193.9 %all-reduce.5.cloned.1.call-done = f32[512,512]{1,0:T(8,128)} async-done(((f32[512,512]{1,0:T(8,128)}), f32[512,512]{1,0:T(8,128)}) %all-reduce.5.cloned.1.call-update) | async-done | bytes 1048592 | tf_op jit(solution)/shard_map/psum | solution.py:12
  407.8 12.7 %fusion.4 = f32[512,512]{1,0:T(8,128)S(1)} fusion(f32[512,512]{1,0:T(8,128)} %all-reduce.5.cloned.1.call-done, f32[512,512]{0,1:T(8,128)S(1)} %fusion.1, f32[512]{0:T(512)S(1)} %add_rsqrt_fusion, f32[512]{0:T(512)S(1)} %add_rsqrt_fusion.1), kind=kOutput, calls=%fused_computation.10 | convolution fusion | flops 1620574208 | bytes 3149824 | tf_op jit(solution)/shard_map/dot_general | solution.py:36
  420.5 67.7 %all-gather.3.cloned.1.call-done = bf16[128,4,1024]{2,1,0:T(4,128)(2,1)} async-done(((bf16[1,4,1024]{2,1,0:T(4,128)(2,1)}), bf16[128,4,1024]{2,1,0:T(4,128)(2,1)}) %all-gather.3.cloned.1.call-update) | async-done | bytes 1048592 | tf_op jit(solution)/shard_map/all_gather | solution.py:56
  488.2 1.3 reshape.15
  489.6 0.3 multiply_reduce_fusion.2
  489.8 0.0 copy-start.4
  489.9 0.7 fusion.3
  490.6 0.5 copy-done.4
  491.1 0.0 copy-start.1
  491.1 11.5 %fusion.52 = f32[512,512]{1,0:T(8,128)S(1)} fusion(f32[512,512]{1,0:T(8,128)S(1)} %copy-done.4, f32[512,512]{0,1:T(8,128)S(1)} %fusion.3, f32[512]{0:T(512)S(1)} %add_rsqrt_fusion.1, f32[512]{0:T(512)S(1)} %add_rsqrt_fusion.2), kind=kOutput, calls=%fused_computation.58 | convolution fusion | flops 1620574208 | bytes 3149824 | tf_op jit(solution)/shard_map/dot_general | solution.py:36
  502.6 0.0 copy-done.1
  502.6 2.8 subtract_select_fusion
  (3 shorter events, 0.0 us)
Async XLA Ops:
  6.5 205.0 %all-reduce.3.cloned.1.call-start = ((), (), s32[]{:S(2)}) async-start(), calls=%async_computation | async-start | bytes 2097152 | tf_op jit(solution)/shard_map/psum | solution.py:12
  9.5 1.2 copy-start.2
  9.6 398.3 %all-reduce.5.cloned.1.call-start = ((), (), s32[]{:S(2)}) async-start(), calls=%async_computation.1 | async-start | bytes 2097152 | tf_op jit(solution)/shard_map/psum | solution.py:12
  11.8 0.8 copy-start.5
  11.8 2.0 copy-start
  11.9 476.3 %all-gather.3.cloned.1.call-start = ((), (), s32[]{:S(2)}) async-start(), calls=%async_computation.2 | async-start | bytes 1056768 | tf_op jit(solution)/shard_map/all_gather | solution.py:56
  211.6 1.6 copy-start.3
  489.8 1.2 copy-start.4
  491.1 11.5 %copy-start.1 = (f32[512,512]{1,0:T(8,128)S(1)}, f32[512,512]{1,0:T(8,128)}, u32[]{:S(2)}) copy-start(f32[512,512]{1,0:T(8,128)} %param.9) | copy-start | bytes 3145732
Sparse Core Ops, SparseCore 0:
  10.6 200.9 all-reduce.2
  214.8 193.0 all-reduce.4
  410.9 77.2 all-gather.2
where the time goes:
time: 512 us
  waiting for transfers between devices  460 us (90%)
  matrix products  28.5 us (6%)
  between operations  14.5 us (3%)
  other arithmetic  5.59 us (1%)
    psum x2, waiting for transfers between devices, broadcast(): return lax.psum(jnp.where(mine, shard, jnp.zeros_like(shard)), axis)  391 us
    all_gather x1, waiting for transfers between devices, on_device(): lax.all_gather(centres_rows, 'col', axis=0, tiled=True)  67.7 us
    dot_general x2, matrix products, apply_inverse(): lax.dot_general(values, inverse, (((1,), (1,)), ((), ())), precision=lax....  24.2 us
  transfers between devices with their start and end apart: 3, of which 3 were waited for; matrix products, arithmetic and copies ran while one was open for 3% of the time, Pallas kernels for 0%

commit v1 on v0

--- a/solution.py
+++ b/solution.py
@@ -53,7 +53,12 @@
     def panel_rows_of(piece):
         return apply_inverse(kernel(piece, panel_x), panel_inv)
 
-    rows_l = panel_rows_of(lax.all_gather(centres_rows, "col", axis=0, tiled=True))
+    def work_strings(state, comm_axis="col"):
+        placed = jnp.stack([state for _ in range(lax.axis_size(comm_axis))], 0)
+        answer = lax.all_to_all(placed, comm_axis, 0, 0)
+        return jnp.concatenate(answer, 0)
+
+    rows_l = panel_rows_of(work_strings(centres_rows))
     cols_l = panel_rows_of(centres_cols)
     update = lax.dot_general(
         rows_l,

time: 512 us -> 464 us (0.906)
  waiting for transfers between devices: 460 us -> 388 us
  starting transfers between devices: 0.09 us -> 18.8 us
    all_gather x1 -> x0, waiting for transfers between devices: 67.7 us -> none  [on_device(): lax.all_gather(centres_rows, 'col', axis=0, tiled=True)]
    all_to_all x0 -> x1, starting transfers between devices: none -> 18.6 us  [work_strings(): answer = lax.all_to_all(placed, comm_axis, 0, 0)]
  transfers between devices with their start and end apart: 3 -> 3, of which waited for: 3 -> 2; matrix products, arithmetic and copies ran while one was open for 3% -> 4% of each run, Pallas kernels for 0% -> 0%
where the time goes in v1:
time: 464 us; the launch traced here: 463 us
  waiting for transfers between devices  388 us (84%)
  matrix products  30.9 us (7%)
  starting transfers between devices  18.8 us (4%)
  between operations  14.8 us (3%)
  other arithmetic  5.69 us (1%)
    psum x2, waiting for transfers between devices, broadcast(): return lax.psum(jnp.where(mine, shard, jnp.zeros_like(shard)), axis)  388 us
    dot_general x2, matrix products, apply_inverse(): lax.dot_general(values, inverse, (((1,), (1,)), ((), ())), precision=lax....  24.3 us
    all_to_all x1, starting transfers between devices, work_strings(): answer = lax.all_to_all(placed, comm_axis, 0, 0)  18.6 us
  transfers between devices with their start and end apart: 3, of which 2 were waited for; matrix products, arithmetic and copies ran while one was open for 4% of the time, Pallas kernels for 0%

profile of v1, /device:TPU:1, one launch (start us, length us, event | category | flops | bytes accessed | tf_op | source)
XLA Modules:
  0.0 462.9 jit_solution(11941349508006157494)
XLA Ops:
  6.5 0.0 all-reduce.3.cloned.1.call-start
  6.5 1.3 fusion.110
  8.5 1.1 broadcast_select_fusion
  9.5 0.0 copy-start.4
  9.5 0.0 all-reduce.3.cloned.1.call-update
  9.6 0.7 copy-done.4
  10.2 1.3 stack.2
  11.5 0.0 copy-start.2
  11.6 18.6 %all-to-all-start = ((bf16[128,4,1024]{2,1,0:T(4,128)(2,1)}), bf16[128,4,1024]{2,1,0:T(4,128)(2,1)S(1)}, u32[]{:S(2)}, u32[]{:S(2)}) async-start(bf16[128,4,1024]{2,1,0:T(4,128)(2,1)} %stack.2), calls=%async_computation | async-start | bytes 2097152 | tf_op jit(solution)/shard_map/all_to_all | solution.py:58
  30.1 0.2 all-reduce.5.cloned.1.call-start
  30.3 0.0 copy-done.2
  30.4 1.1 broadcast_select_fusion.1
  31.4 0.0 copy-start.6
  31.4 0.0 copy-start
  31.4 0.0 all-reduce.5.cloned.1.call-update
  31.4 0.6 copy-done.6
  32.1 0.6 dynamic_slice.4
  33.3 0.0 copy-done
  33.3 0.3 multiply_reduce_fusion
  33.6 195.2 %all-reduce.3.cloned.1.call-done = bf16[512,1024]{1,0:T(8,128)(2,1)} async-done(((bf16[512,1024]{1,0:T(8,128)(2,1)}), bf16[512,1024]{1,0:T(8,128)(2,1)}) %all-reduce.3.cloned.1.call-update) | async-done | bytes 1048592 | tf_op jit(solution)/shard_map/psum | solution.py:12
  228.8 0.0 copy-start.3
  228.8 1.6 multiply_reduce_fusion.1
  230.4 0.0 copy-done.3
  230.4 1.7 fusion.1
  232.1 192.9 %all-reduce.5.cloned.1.call-done = f32[512,512]{1,0:T(8,128)} async-done(((f32[512,512]{1,0:T(8,128)}), f32[512,512]{1,0:T(8,128)}) %all-reduce.5.cloned.1.call-update) | async-done | bytes 1048592 | tf_op jit(solution)/shard_map/psum | solution.py:12
  425.1 13.0 %fusion.4 = f32[512,512]{1,0:T(8,128)S(1)} fusion(f32[512,512]{1,0:T(8,128)} %all-reduce.5.cloned.1.call-done, f32[512,512]{0,1:T(8,128)} %fusion.1, f32[512]{0:T(512)S(1)} %add_rsqrt_fusion, f32[512]{0:T(512)S(1)} %add_rsqrt_fusion.1), kind=kOutput, calls=%fused_computation.10 | convolution fusion | flops 1620574208 | bytes 3149824 | tf_op jit(solution)/shard_map/dot_general | solution.py:36
  438.1 0.0 all-to-all-done
  438.1 0.4 multiply_reduce_fusion.2
  438.5 0.1 copy.12
  438.6 0.1 sqrt.31
  438.7 1.1 reshape.26
  439.8 0.0 copy-start.5
  439.9 2.1 fusion.3
  441.9 0.0 copy-done.5
  441.9 0.0 copy-start.1
  441.9 11.3 %fusion.52 = f32[512,512]{1,0:T(8,128)S(1)} fusion(f32[512,512]{1,0:T(8,128)S(1)} %copy-done.5, f32[512,512]{0,1:T(8,128)S(1)} %fusion.3, f32[512]{0:T(512)S(1)} %add_rsqrt_fusion.1, f32[512]{0:T(512)S(1)} %sqrt.31), kind=kOutput, calls=%fused_computation.58 | convolution fusion | flops 1620574208 | bytes 3149824 | tf_op jit(solution)/shard_map/dot_general | solution.py:36
  453.2 0.0 copy-done.1
  453.2 2.8 subtract_select_fusion
  (3 shorter events, 0.0 us)
Async XLA Ops:
  6.5 222.2 %all-reduce.3.cloned.1.call-start = ((), (), s32[]{:S(2)}) async-start(), calls=%async_computation.1 | async-start | bytes 2097152 | tf_op jit(solution)/shard_map/psum | solution.py:12
  9.5 0.7 copy-start.4
  11.5 18.8 %copy-start.2 = (f32[512,512]{1,0:T(8,128)S(1)}, f32[512,512]{1,0:T(8,128)}, u32[]{:S(2)}) copy-start(f32[512,512]{1,0:T(8,128)} %param.8) | copy-start | bytes 3145732
  11.6 426.6 %all-to-all-start = ((bf16[128,4,1024]{2,1,0:T(4,128)(2,1)}), bf16[128,4,1024]{2,1,0:T(4,128)(2,1)S(1)}, u32[]{:S(2)}, u32[]{:S(2)}) async-start(bf16[128,4,1024]{2,1,0:T(4,128)(2,1)} %stack.2), calls=%async_computation | async-start | bytes 2097152 | tf_op jit(solution)/shard_map/all_to_all | solution.py:58
  30.1 395.0 %all-reduce.5.cloned.1.call-start = ((), (), s32[]{:S(2)}) async-start(), calls=%async_computation.2 | async-start | bytes 2097152 | tf_op jit(solution)/shard_map/psum | solution.py:12
  31.4 0.7 copy-start.6
  31.4 1.9 copy-start
  228.8 1.6 copy-start.3
  439.8 2.1 copy-start.5
  441.9 11.3 %copy-start.1 = (f32[512,512]{1,0:T(8,128)S(1)}, f32[512,512]{1,0:T(8,128)}, u32[]{:S(2)}) copy-start(f32[512,512]{1,0:T(8,128)} %param.9) | copy-start | bytes 3145732
Sparse Core Ops, SparseCore 0:
  10.6 218.1 all-reduce.2
  232.0 193.0 all-reduce.4
